TPU v7x, 128 devices: a whole 4x4x4 slice. The times are simulated.
128 devices in a mesh: dp: 32 (over x, z, core), section: 4 (over y).
Axes of the slice: x: 4, y: 4, z: 4, core: 2. Of those that a mesh axis runs over, the one named last changes fastest.
Arguments:
- hidden: bfloat16 [12288, 4096], P('dp'), may hold values from -6 to 6
- encoded: bfloat16 [384, 128, 896], P('dp'), may hold values from -6 to 6
- owner: int32 [32, 12], P('dp'), may hold values from 0 to 5, never falling along the last dimension, each value on 1 to 4 neighbouring positions
- w_query: bfloat16 [4, 4096, 2048], P('section', 'dp'), may hold values from -0.09375 to 0.09375
- w_key: bfloat16 [4, 896, 2048], P('section'), may hold values from -0.1875 to 0.1875
- w_value: bfloat16 [4, 896, 2048], P('section'), may hold values from -0.1875 to 0.1875
- w_out: bfloat16 [4, 2048, 4096], P('section', None, 'dp'), may hold values from -0.75 to 0.75
Outputs:
- layer_outputs: bfloat16 [4, 12288, 4096], P('section', 'dp')
Inputs may be any that keep to these rules, and one draw needn't show every extreme that they name: owner[g] lists for each of dp index g's 12 neighbours the span of g it was retrieved for; the list never falls, every span owns 1 to 4 neighbours and some span exactly 4.
All inputs are finite; a program needn't handle non-finite values.
Results may differ from a plain program's by a relative error of at most 0.028.
Values may be sent and summed in bfloat16 or wider, within the bound.
No kernel may reach another device: no remote copies, remote signals or barrier semaphores. Data moves between devices by JAX's collectives and lax.ppermute only.
A program may use at most 384 MiB of HBM per device.

v0:
```python
import jax
import jax.numpy as jnp
from jax import lax
from jax.sharding import PartitionSpec as P

HEADS = 16
HDIM = 128
SPAN = 64
NBR_LEN = 128
MOST = 4
epsilon = 1e-05


def from_behind(block, axis, distance):
    devices = range(lax.axis_size(axis))
    route = [(i - distance, i) for i in devices if i - distance in devices]
    return lax.ppermute(block, axis, route)


def attend_all(query_heads, key_flat, value_flat, owners, span_ids):
    scores = jnp.einsum(
        "cthd,khd->chtk", query_heads, key_flat, preferred_element_type=jnp.float32
    ) * (1.0 / HDIM**0.5)
    belongs = jnp.repeat(owners[None, :] == span_ids[:, None], NBR_LEN, axis=1)
    weights = jnp.where(belongs[:, None, None, :], jnp.exp(scores), 0.0)
    denominator = jnp.sum(weights, axis=3, keepdims=True)
    weights_low = (weights / denominator).astype(jnp.bfloat16)
    return jnp.einsum(
        "chtk,khd->cthd", weights_low, value_flat, preferred_element_type=jnp.float32
    ).astype(jnp.bfloat16)


def prepare_keys(rows_enc, key_mat, value_mat, head_count):
    key_rows = jnp.dot(rows_enc, key_mat, preferred_element_type=jnp.float32).astype(jnp.bfloat16)
    value_rows = jnp.dot(rows_enc, value_mat, preferred_element_type=jnp.float32).astype(
        jnp.bfloat16
    )
    nbr_count = rows_enc.shape[0] // NBR_LEN
    padding = jnp.zeros((MOST, NBR_LEN, head_count, HDIM), jnp.bfloat16)
    key_blocks = jnp.concatenate(
        [key_rows.reshape(nbr_count, NBR_LEN, head_count, HDIM), padding], axis=0
    )
    value_blocks = jnp.concatenate(
        [value_rows.reshape(nbr_count, NBR_LEN, head_count, HDIM), padding], axis=0
    )
    key_flat = key_rows.reshape(nbr_count * NBR_LEN, head_count, HDIM)
    value_flat = value_rows.reshape(nbr_count * NBR_LEN, head_count, HDIM)
    return (key_blocks, value_blocks, key_flat, value_flat)


def attend(query_heads, key_pack, owners, span_ids):
    return attend_all(query_heads, key_pack[2], key_pack[3], owners, span_ids)


def per_device(hidden, encoded, owner, w_query, w_key, w_value, w_out):
    section_id = lax.axis_index("section")
    section_count = lax.axis_size("section")
    enc_width = encoded.shape[2]
    model_width = hidden.shape[1]
    rows_enc = encoded.reshape(-1, enc_width)
    owners = owner[0]
    query_full, out_full = (
        lax.all_gather(w_query, "dp", axis=1, tiled=True),
        lax.all_gather(w_out, "dp", axis=2, tiled=True),
    )
    query_mat = query_full[0]
    out_mat = out_full[0]
    own_pack = prepare_keys(rows_enc, w_key[0], w_value[0], HEADS)
    span_count = hidden.shape[0] // SPAN
    every_span = jnp.arange(span_count, dtype=jnp.int32)
    current = hidden
    stored = jnp.zeros_like(hidden)
    for step_index in range(section_count):
        if step_index > 0:
            current = from_behind(current, "section", 1)
        active = section_id == step_index
        row_count = current.shape[0]
        widened = current.astype(jnp.float32)
        normed = (
            widened * lax.rsqrt(jnp.mean(widened * widened, axis=-1, keepdims=True) + epsilon)
        ).astype(jnp.bfloat16)
        empty = jnp.zeros((row_count, model_width), jnp.float32)

        def heavy_full(operand):
            queries = jnp.dot(operand, query_mat, preferred_element_type=jnp.float32).astype(
                jnp.bfloat16
            )
            query_heads = queries.reshape(every_span.shape[0], SPAN, HEADS, HDIM)
            attended = attend(query_heads, own_pack, owners, every_span)
            return jnp.dot(
                attended.reshape(row_count, HEADS * HDIM),
                out_mat,
                preferred_element_type=jnp.float32,
            )

        def light_full(operand):
            return empty

        branch = lax.cond(active, heavy_full, light_full, normed)
        result = (widened + branch).astype(jnp.bfloat16)
        current = jnp.where(active, result, current)
        stored = jnp.where(active, result, stored)
    return stored[None]


def solution(mesh):
    placed = (
        P("dp", None),
        P("dp", None, None),
        P("dp", None),
        P("section", "dp", None),
        P("section", None, None),
        P("section", None, None),
        P("section", None, "dp"),
    )
    return jax.shard_map(
        per_device, mesh=mesh, in_specs=placed, out_specs=P("section", "dp", None), check_vma=False
    )
```

profile of v0, /device:TPU:24, one launch (start us, length us, event | category | flops | bytes accessed | tf_op | source)
XLA Modules:
  0.0 728.9 jit_solution(6954939730521494805)
XLA Ops:
  8.3 9.1 %fusion.111 = bf16[192,8,16,128]{3,1,2,0:T(8,128)(2,1)S(1)} fusion(bf16[1536,896]{1,0:T(8,128)(2,1)S(1)} %bitcast.152, bf16[1,896,2048]{2,1,0:T(8,128)(2,1)} %param.20), kind=kOutput, calls=%fused_computation.118 | convolution fusion | flops 5640290304 | bytes 12713984 | tf_op jit(solution)/shard_map/dot_general | solution.py:35
  17.4 5.0 copy.73
  22.4 7.2 fusion.108
  29.6 5.0 copy.72
  38.0 46.4 %all-gather.3.cloned.1.call-done = bf16[1,4096,2048]{2,1,0:T(8,128)(2,1)} async-done(((bf16[1,128,2048]{2,1,0:T(8,128)(2,1)}), bf16[1,4096,2048]{2,1,0:T(8,128)(2,1)}) %all-gather.3.cloned.1.call-update) | async-done | bytes 16777232 | tf_op jit(solution)/shard_map/all_gather | solution.py:63
  84.4 82.8 %all-gather.5.cloned.1.call-done = bf16[1,2048,4096]{2,1,0:T(8,128)(2,1)} async-done(((bf16[1,2048,128]{2,1,0:T(8,128)(2,1)}), bf16[1,2048,4096]{2,1,0:T(8,128)(2,1)}) %all-gather.5.cloned.1.call-update) | async-done | bytes 16777232 | tf_op jit(solution)/shard_map/all_gather | solution.py:64
  167.2 11.7 %conditional.4 = (f32[384,4096]{1,0:T(8,128)}) conditional(s32[]{:T(128)} %convert_element_type.103, () %tuple.29, (s32[1,12]{1,0:T(1,128)S(1)}, s32[6]{0:T(128)S(1)}, bf16[384,4096]{1,0:T(8,128)(2,1)}, bf16[4096,2048]{1,0:T(8,128)(2,1)}, bf16[1536,16,128]{2,1,0:T(8,128)(2,1)}, /*index=5*/bf16[1536,16,128]{2,1,0:T(8,128)(2,1)}, ...), branch_computations={%region_1.0_spmd, %region_2.4_spmd} | conditional | flops 17784367104 | bytes 143750368 | solution.py:99
  178.9 7.8 %broadcast_select_fusion = bf16[384,4096]{1,0:T(8,128)(2,1)} fusion(bf16[384,4096]{1,0:T(8,128)(2,1)} %param.15, pred[]{:T(512)S(6)} %eq.75, f32[384,4096]{1,0:T(8,128)} %get-tuple-element.165), kind=kLoop, calls=%fused_computation.114 | loop fusion | flops 6291456 | bytes 12582913 | tf_op jit(solution)/shard_map/jit(_where)/select_n | solution.py:101
  188.0 71.2 %collective-permute-done = bf16[384,4096]{1,0:T(8,128)(2,1)} collective-permute-done((bf16[384,4096]{1,0:T(8,128)(2,1)}, bf16[384,4096]{1,0:T(8,128)(2,1)}, u32[]{:S(2)}, u32[]{:S(2)}) %collective-permute-start) | collective-permute-done | bytes 3145760 | tf_op jit(solution)/shard_map/ppermute | solution.py:17
  261.8 4.6 fusion.96
  266.4 11.8 %conditional.5 = (f32[384,4096]{1,0:T(8,128)}) conditional(s32[]{:T(128)} %convert_element_type.109, () %tuple.31, (s32[1,12]{1,0:T(1,128)S(1)}, s32[6]{0:T(128)S(1)}, bf16[384,4096]{1,0:T(8,128)(2,1)}, bf16[4096,2048]{1,0:T(8,128)(2,1)}, bf16[1536,16,128]{2,1,0:T(8,128)(2,1)}, /*index=5*/bf16[1536,16,128]{2,1,0:T(8,128)(2,1)}, ...), branch_computations={%region_5.6_spmd, %region_6.8_spmd} | conditional | flops 17784367104 | bytes 143750368 | solution.py:99
  278.2 7.8 %broadcast_select_fusion.1 = bf16[384,4096]{1,0:T(8,128)(2,1)} fusion(bf16[384,4096]{1,0:T(8,128)(2,1)} %collective-permute-done, pred[]{:T(512)S(6)} %eq.74, f32[384,4096]{1,0:T(8,128)} %get-tuple-element.166), kind=kLoop, calls=%fused_computation.115 | loop fusion | flops 6291456 | bytes 12582913 | tf_op jit(solution)/shard_map/jit(_where)/select_n | solution.py:101
  287.3 70.4 %collective-permute-done.1 = bf16[384,4096]{1,0:T(8,128)(2,1)} collective-permute-done((bf16[384,4096]{1,0:T(8,128)(2,1)}, bf16[384,4096]{1,0:T(8,128)(2,1)}, u32[]{:S(2)}, u32[]{:S(2)}) %collective-permute-start.1) | collective-permute-done | bytes 3145760 | tf_op jit(solution)/shard_map/ppermute | solution.py:17
  360.2 4.6 fusion.99
  364.8 11.8 %conditional.6 = (f32[384,4096]{1,0:T(8,128)}) conditional(s32[]{:T(128)} %convert_element_type.113, () %tuple.33, (s32[1,12]{1,0:T(1,128)S(1)}, s32[6]{0:T(128)S(1)}, bf16[384,4096]{1,0:T(8,128)(2,1)}, bf16[4096,2048]{1,0:T(8,128)(2,1)}, bf16[1536,16,128]{2,1,0:T(8,128)(2,1)}, /*index=5*/bf16[1536,16,128]{2,1,0:T(8,128)(2,1)}, ...), branch_computations={%region_9.10_spmd, %region_10.12_spmd} | conditional | flops 17784367104 | bytes 143750368 | solution.py:99
  376.7 7.9 %broadcast_select_fusion.2 = bf16[384,4096]{1,0:T(8,128)(2,1)} fusion(bf16[384,4096]{1,0:T(8,128)(2,1)} %collective-permute-done.1, pred[]{:T(512)S(6)} %eq.73, f32[384,4096]{1,0:T(8,128)} %get-tuple-element.167), kind=kLoop, calls=%fused_computation.116 | loop fusion | flops 6291456 | bytes 12582913 | tf_op jit(solution)/shard_map/jit(_where)/select_n | solution.py:101
  385.9 242.9 %collective-permute-done.2 = bf16[384,4096]{1,0:T(8,128)(2,1)} collective-permute-done((bf16[384,4096]{1,0:T(8,128)(2,1)}, bf16[384,4096]{1,0:T(8,128)(2,1)}, u32[]{:S(2)}, u32[]{:S(2)}) %collective-permute-start.2) | collective-permute-done | bytes 3145760 | tf_op jit(solution)/shard_map/ppermute | solution.py:17
  631.4 4.6 fusion.102
  636.0 70.3 %conditional.7 = (f32[384,4096]{1,0:T(8,128)}) conditional(s32[]{:T(128)} %convert_element_type.117, () %tuple.35, (s32[1,12]{1,0:T(1,128)S(1)}, s32[6]{0:T(128)S(1)}, bf16[384,4096]{1,0:T(8,128)(2,1)}, bf16[4096,2048]{1,0:T(8,128)(2,1)}, bf16[1536,16,128]{2,1,0:T(8,128)(2,1)}, /*index=5*/bf16[1536,16,128]{2,1,0:T(8,128)(2,1)}, ...), branch_computations={%region_13.14_spmd, %region_14.16_spmd} | conditional | flops 17784367104 | bytes 143750368 | solution.py:99
  636.1 11.1 %fusion.84 = bf16[48,8,16,128]{3,1,2,0:T(8,128)(2,1)S(1)} fusion(bf16[384,4096]{1,0:T(8,128)(2,1)} %get-tuple-element.96, bf16[4096,2048]{1,0:T(8,128)(2,1)} %get-tuple-element.97), kind=kOutput, calls=%fused_computation.77 | convolution fusion | flops 6443237376 | bytes 21495808 | tf_op jit(solution)/shard_map/cond/branch_1_fun/dot_general | solution.py:85
  647.7 24.3 %bitcast_reduce_fusion.3 = (f32[6,16,64]{2,0,1:T(8,128)S(1)}, f32[16,6,64,1536]{3,2,1,0:T(8,128)}) fusion(pred[6,1536]{1,0:T(8,128)(4,1)S(1)} %bitcast.183, bf16[1536,16,128,1]{2,1,0,3:T(8,128)(2,1)} %bitcast.168, bf16[6,64,16,128]{3,2,1,0:T(8,128)(2,1)S(1)} %bitcast.172), kind=kOutput, calls=%fused_computation.64 | convolution fusion | flops 2444224512 | bytes 45646848 | tf_op jit(solution)/shard_map/cond/branch_1_fun/cthd,khd->chtk/dot_general | solution.py:21
  672.0 21.1 %fusion.85 = bf16[6,64,16,128]{3,1,0,2:T(8,128)(2,1)S(1)} fusion(bf16[1536,16,128,1]{2,1,0,3:T(8,128)(2,1)} %bitcast.160, f32[16,6,64,1536]{3,2,1,0:T(8,128)} %get-tuple-element.164, f32[6,16,64]{2,0,1:T(8,128)S(1)} %get-tuple-element.163, pred[6,1536]{1,0:T(8,128)(4,1)S(1)} %bitcast.184), kind=kOutput, calls=%fused_computation.78 | convolution fusion | flops 2454454272 | bytes 45646848 | tf_op jit(solution)/shard_map/cond/branch_1_fun/chtk,khd->cthd/dot_general | solution.py:28
  694.1 11.9 %fusion.80 = f32[384,4096]{1,0:T(8,128)} fusion(bf16[2048,4096]{1,0:T(8,128)(2,1)} %get-tuple-element.100, bf16[48,8,16,128]{3,2,1,0:T(8,128)(2,1)S(1)} %bitcast.176), kind=kOutput, calls=%fused_computation.73 | convolution fusion | flops 6442450944 | bytes 24641536 | tf_op jit(solution)/shard_map/cond/branch_1_fun/dot_general | solution.py:90
  706.3 15.6 %fusion.107 = bf16[1,384,4096]{2,1,0:T(8,128)(2,1)} fusion(f32[384,4096]{1,0:T(8,128)} %get-tuple-element.168, bf16[384,4096]{1,0:T(8,128)(2,1)} %collective-permute-done.2, pred[]{:T(512)S(6)} %eq.75, pred[]{:T(512)S(6)} %eq.74, pred[]{:T(512)S(6)} %eq.73, pred[]{:T(512)S(6)} %eq.72, f32[384,4096]{1,0:T(8,128)} %get-tuple-element.167, ...), kind=kLoop, calls=%fused_computation.113 | loop fusion | flops 25165824 | bytes 40894468 | tf_op jit(solution)/shard_map/broadcast_in_dim | solution.py:103
  (38 shorter events, 28.5 us)
Async XLA Ops:
  6.5 1.8 copy-start
  6.5 77.8 %all-gather.3.cloned.1.call-start = ((), (), s32[]{:S(2)}) async-start(), calls=%async_computation | async-start | bytes 17301504 | tf_op jit(solution)/shard_map/all_gather | solution.py:63
  7.3 159.9 %all-gather.5.cloned.1.call-start = ((), (), s32[]{:S(2)}) async-start(), calls=%async_computation.1 | async-start | bytes 17301504 | tf_op jit(solution)/shard_map/all_gather | solution.py:64
  17.4 5.0 copy-start.4
  29.6 5.0 copy-start.2
  34.6 132.6 %copy-start.3 = (s32[1,12]{1,0:T(1,128)S(1)}, s32[1,12]{1,0:T(1,128)}, u32[]{:S(2)}) copy-start(s32[1,12]{1,0:T(1,128)} %param.17) | copy-start | bytes 148
  186.7 72.5 %collective-permute-start = (bf16[384,4096]{1,0:T(8,128)(2,1)}, bf16[384,4096]{1,0:T(8,128)(2,1)}, u32[]{:S(2)}, u32[]{:S(2)}) collective-permute-start(bf16[384,4096]{1,0:T(8,128)(2,1)} %broadcast_select_fusion), channel_id=1, source_target_pairs={{0,1},{1,2},{2,3},{4,5},{5,6},{6,7},{8,9},{9,10},{10,11},{12,13},{... | collective-permute-start | bytes 9437192 | tf_op jit(solution)/shard_map/ppermute | solution.py:17
  286.0 71.7 %collective-permute-start.1 = (bf16[384,4096]{1,0:T(8,128)(2,1)}, bf16[384,4096]{1,0:T(8,128)(2,1)}, u32[]{:S(2)}, u32[]{:S(2)}) collective-permute-start(bf16[384,4096]{1,0:T(8,128)(2,1)} %broadcast_select_fusion.1), channel_id=1, source_target_pairs={{0,1},{1,2},{2,3},{4,5},{5,6},{6,7},{8,9},{9,10},{10,11},{12,13},{... | collective-permute-start | bytes 9437192 | tf_op jit(solution)/shard_map/ppermute | solution.py:17
  384.6 244.2 %collective-permute-start.2 = (bf16[384,4096]{1,0:T(8,128)(2,1)}, bf16[384,4096]{1,0:T(8,128)(2,1)}, u32[]{:S(2)}, u32[]{:S(2)}) collective-permute-start(bf16[384,4096]{1,0:T(8,128)(2,1)} %broadcast_select_fusion.2), channel_id=1, source_target_pairs={{0,1},{1,2},{2,3},{4,5},{5,6},{6,7},{8,9},{9,10},{10,11},{12,13},{... | collective-permute-start | bytes 9437192 | tf_op jit(solution)/shard_map/ppermute | solution.py:17
  706.2 15.6 %copy-start.1 = (bf16[12,128,896]{2,1,0:T(8,128)(2,1)S(1)}, bf16[12,128,896]{2,1,0:T(8,128)(2,1)}, u32[]{:S(2)}) copy-start(bf16[12,128,896]{2,1,0:T(8,128)(2,1)} %param.16) | copy-start | bytes 8257540
Sparse Core Ops, SparseCore 0:
  9.6 74.6 all-gather.2
  86.5 80.5 all-gather.4
where the time goes:
time: 736 us; the launch traced here: 729 us
  waiting for transfers between devices  515 us (70%)
  matrix products  84.7 us (12%)
  other arithmetic  64.1 us (9%)
  loops' own time  25.4 us (3%)
  local copies, waits for them, and re-layouts  22 us (3%)
  between operations  13.8 us (2%)
    ppermute x3, waiting for transfers between devices, from_behind(): return lax.ppermute(block, axis, route)  384 us
    all_gather x1, waiting for transfers between devices, per_device(): lax.all_gather(w_out, 'dp', axis=2, tiled=True)  82.8 us
    all_gather x1, waiting for transfers between devices, per_device(): lax.all_gather(w_query, 'dp', axis=1, tiled=True)  46.4 us
    another operation x4, loops' own time, per_device(): branch = lax.cond(active, heavy_full, light_full, normed)  25.4 us
    dot_general x1, matrix products, attend_all(): jnp.einsum('cthd,khd->chtk', query_heads, key_flat, preferred_element_typ...  24.3 us
    select_n x3, other arithmetic, per_device(): current = jnp.where(active, result, current)  23.6 us
    dot_general x1, matrix products, attend_all(): jnp.einsum('chtk,khd->cthd', weights_low, value_flat, preferred_element_t...  21.1 us
    convert_element_type x4, other arithmetic, per_device(): normed = (widened * lax.rsqrt(jnp.mean(widened * widened, axis=-1, keepdi...  16.4 us
  transfers between devices with their start and end apart: 5, of which 5 were waited for; matrix products, arithmetic and copies ran while one was open for 4% of the time, Pallas kernels for 0%

commit v1 on v0

--- a/solution.py
+++ b/solution.py
@@ -60,7 +60,9 @@
     rows_enc = encoded.reshape(-1, enc_width)
     owners = owner[0]
     query_full, out_full = (
-        lax.all_gather(w_query, "dp", axis=1, tiled=True),
+        jnp.concatenate(
+            lax.all_to_all(jnp.stack([w_query] * lax.axis_size("dp")), "dp", 0, 0), axis=1
+        ),
         lax.all_gather(w_out, "dp", axis=2, tiled=True),
     )
     query_mat = query_full[0]

time: 736 us -> 872 us (1.18)
  the two profiles are of different devices: /device:TPU:24 before, /device:TPU:60 now
where the time goes in v1:
time: 872 us; the launch traced here: 865 us
  waiting for transfers between devices  637 us (73%)
  matrix products  84.8 us (10%)
  other arithmetic  64.1 us (7%)
  local copies, waits for them, and re-layouts  28.5 us (3%)
  loops' own time  25.4 us (3%)
  between operations  13.8 us (2%)
  starting transfers between devices  11.9 us (1%)
    ppermute x3, waiting for transfers between devices, from_behind(): return lax.ppermute(block, axis, route)  384 us
    all_to_all x1, waiting for transfers between devices, per_device(): lax.all_to_all(jnp.stack([w_query] * lax.axis_size('dp')), 'dp', 0, 0)  252 us
    another operation x4, loops' own time, per_device(): branch = lax.cond(active, heavy_full, light_full, normed)  25.4 us
    dot_general x1, matrix products, attend_all(): jnp.einsum('cthd,khd->chtk', query_heads, key_flat, preferred_element_typ...  24.2 us
    select_n x3, other arithmetic, per_device(): current = jnp.where(active, result, current)  23.6 us
    dot_general x1, matrix products, attend_all(): jnp.einsum('chtk,khd->cthd', weights_low, value_flat, preferred_element_t...  21.1 us
  transfers between devices with their start and end apart: 5, of which 4 were waited for; matrix products, arithmetic and copies ran while one was open for 4% of the time, Pallas kernels for 0%

profile of v1, /device:TPU:60, one launch (start us, length us, event | category | flops | bytes accessed | tf_op | source)
XLA Modules:
  0.0 865.2 jit_solution(10456389897315666247)
XLA Ops:
  7.3 6.8 stack.2
  14.1 8.0 all-to-all-start
  22.2 9.2 %fusion.111 = bf16[192,8,16,128]{3,1,2,0:T(8,128)(2,1)S(1)} fusion(bf16[1536,896]{1,0:T(8,128)(2,1)S(1)} %bitcast.153, bf16[1,896,2048]{2,1,0:T(8,128)(2,1)} %param.20), kind=kOutput, calls=%fused_computation.118 | convolution fusion | flops 5640290304 | bytes 12713984 | tf_op jit(solution)/shard_map/dot_general | solution.py:35
  31.4 5.0 copy.89
  36.4 7.2 fusion.108
  43.6 5.0 copy.88
  52.0 251.9 %all-to-all-done = bf16[32,1,128,2048]{3,2,1,0:T(8,128)(2,1)} async-done(((bf16[32,1,128,2048]{3,2,1,0:T(8,128)(2,1)}), bf16[32,1,128,2048]{3,2,1,0:T(8,128)(2,1)}, u32[]{:S(2)}, u32[]{:S(2)}) %all-to-all-start) | async-done | bytes 16777248 | tf_op jit(solution)/shard_map/all_to_all | solution.py:64
  303.8 11.7 %conditional.4 = (f32[384,4096]{1,0:T(8,128)}) conditional(s32[]{:T(128)} %convert_element_type.103, () %tuple.29, (s32[1,12]{1,0:T(1,128)S(1)}, s32[6]{0:T(128)S(1)}, bf16[384,4096]{1,0:T(8,128)(2,1)}, bf16[4096,2048]{1,0:T(8,128)(2,1)}, bf16[1536,16,128]{2,1,0:T(8,128)(2,1)}, /*index=5*/bf16[1536,16,128]{2,1,0:T(8,128)(2,1)}, ...), branch_computations={%region_1.0_spmd, %region_2.4_spmd} | conditional | flops 17784367104 | bytes 143750368 | solution.py:101
  315.6 7.8 broadcast_select_fusion
  324.7 70.8 %collective-permute-done = bf16[384,4096]{1,0:T(8,128)(2,1)} collective-permute-done((bf16[384,4096]{1,0:T(8,128)(2,1)}, bf16[384,4096]{1,0:T(8,128)(2,1)}, u32[]{:S(2)}, u32[]{:S(2)}) %collective-permute-start) | collective-permute-done | bytes 3145760 | tf_op jit(solution)/shard_map/ppermute | solution.py:17
  398.1 4.6 fusion.96
  402.7 11.8 %conditional.5 = (f32[384,4096]{1,0:T(8,128)}) conditional(s32[]{:T(128)} %convert_element_type.109, () %tuple.31, (s32[1,12]{1,0:T(1,128)S(1)}, s32[6]{0:T(128)S(1)}, bf16[384,4096]{1,0:T(8,128)(2,1)}, bf16[4096,2048]{1,0:T(8,128)(2,1)}, bf16[1536,16,128]{2,1,0:T(8,128)(2,1)}, /*index=5*/bf16[1536,16,128]{2,1,0:T(8,128)(2,1)}, ...), branch_computations={%region_5.6_spmd, %region_6.8_spmd} | conditional | flops 17784367104 | bytes 143750368 | solution.py:101
  414.5 7.8 broadcast_select_fusion.1
  423.6 70.0 %collective-permute-done.1 = bf16[384,4096]{1,0:T(8,128)(2,1)} collective-permute-done((bf16[384,4096]{1,0:T(8,128)(2,1)}, bf16[384,4096]{1,0:T(8,128)(2,1)}, u32[]{:S(2)}, u32[]{:S(2)}) %collective-permute-start.1) | collective-permute-done | bytes 3145760 | tf_op jit(solution)/shard_map/ppermute | solution.py:17
  496.2 4.6 fusion.99
  500.7 11.8 %conditional.6 = (f32[384,4096]{1,0:T(8,128)}) conditional(s32[]{:T(128)} %convert_element_type.113, () %tuple.33, (s32[1,12]{1,0:T(1,128)S(1)}, s32[6]{0:T(128)S(1)}, bf16[384,4096]{1,0:T(8,128)(2,1)}, bf16[4096,2048]{1,0:T(8,128)(2,1)}, bf16[1536,16,128]{2,1,0:T(8,128)(2,1)}, /*index=5*/bf16[1536,16,128]{2,1,0:T(8,128)(2,1)}, ...), branch_computations={%region_9.10_spmd, %region_10.12_spmd} | conditional | flops 17784367104 | bytes 143750368 | solution.py:101
  512.6 7.9 broadcast_select_fusion.2
  521.8 243.3 %collective-permute-done.2 = bf16[384,4096]{1,0:T(8,128)(2,1)} collective-permute-done((bf16[384,4096]{1,0:T(8,128)(2,1)}, bf16[384,4096]{1,0:T(8,128)(2,1)}, u32[]{:S(2)}, u32[]{:S(2)}) %collective-permute-start.2) | collective-permute-done | bytes 3145760 | tf_op jit(solution)/shard_map/ppermute | solution.py:17
  772.3 70.2 %conditional.7 = (f32[384,4096]{1,0:T(8,128)}) conditional(s32[]{:T(128)} %convert_element_type.117, () %tuple.35, (s32[1,12]{1,0:T(1,128)S(1)}, s32[6]{0:T(128)S(1)}, bf16[384,4096]{1,0:T(8,128)(2,1)}, bf16[4096,2048]{1,0:T(8,128)(2,1)}, bf16[1536,16,128]{2,1,0:T(8,128)(2,1)}, /*index=5*/bf16[1536,16,128]{2,1,0:T(8,128)(2,1)}, ...), branch_computations={%region_13.14_spmd, %region_14.16_spmd} | conditional | flops 17784367104 | bytes 143750368 | solution.py:101
  772.4 11.1 %fusion.84 = bf16[48,8,16,128]{3,1,2,0:T(8,128)(2,1)S(1)} fusion(bf16[384,4096]{1,0:T(8,128)(2,1)} %get-tuple-element.96, bf16[4096,2048]{1,0:T(8,128)(2,1)} %get-tuple-element.97), kind=kOutput, calls=%fused_computation.77 | convolution fusion | flops 6443237376 | bytes 21495808 | tf_op jit(solution)/shard_map/cond/branch_1_fun/dot_general | solution.py:87
  784.0 24.2 %bitcast_reduce_fusion.3 = (f32[6,16,64]{2,0,1:T(8,128)S(1)}, f32[16,6,64,1536]{3,2,1,0:T(8,128)}) fusion(pred[6,1536]{1,0:T(8,128)(4,1)S(1)} %bitcast.185, bf16[1536,16,128,1]{2,1,0,3:T(8,128)(2,1)} %bitcast.169, bf16[6,64,16,128]{3,2,1,0:T(8,128)(2,1)S(1)} %bitcast.173), kind=kOutput, calls=%fused_computation.64 | convolution fusion | flops 2444224512 | bytes 45646848 | tf_op jit(solution)/shard_map/cond/branch_1_fun/cthd,khd->chtk/dot_general | solution.py:21
  808.3 21.1 %fusion.85 = bf16[6,64,16,128]{3,1,0,2:T(8,128)(2,1)S(1)} fusion(bf16[1536,16,128,1]{2,1,0,3:T(8,128)(2,1)} %bitcast.161, f32[16,6,64,1536]{3,2,1,0:T(8,128)} %get-tuple-element.192, f32[6,16,64]{2,0,1:T(8,128)S(1)} %get-tuple-element.191, pred[6,1536]{1,0:T(8,128)(4,1)S(1)} %bitcast.186), kind=kOutput, calls=%fused_computation.78 | convolution fusion | flops 2454454272 | bytes 45646848 | tf_op jit(solution)/shard_map/cond/branch_1_fun/chtk,khd->cthd/dot_general | solution.py:28
  830.4 11.9 %fusion.80 = f32[384,4096]{1,0:T(8,128)} fusion(bf16[2048,4096]{1,0:T(8,128)(2,1)} %get-tuple-element.100, bf16[48,8,16,128]{3,2,1,0:T(8,128)(2,1)S(1)} %bitcast.177), kind=kOutput, calls=%fused_computation.73 | convolution fusion | flops 6442450944 | bytes 24641536 | tf_op jit(solution)/shard_map/cond/branch_1_fun/dot_general | solution.py:92
  842.5 15.6 %fusion.107 = bf16[1,384,4096]{2,1,0:T(8,128)(2,1)} fusion(f32[384,4096]{1,0:T(8,128)} %get-tuple-element.196, bf16[384,4096]{1,0:T(8,128)(2,1)} %collective-permute-done.2, pred[]{:T(512)S(6)} %eq.75, pred[]{:T(512)S(6)} %eq.74, pred[]{:T(512)S(6)} %eq.73, pred[]{:T(512)S(6)} %eq.72, f32[384,4096]{1,0:T(8,128)} %get-tuple-element.195, ...), kind=kLoop, calls=%fused_computation.113 | loop fusion | flops 25165824 | bytes 40894468 | tf_op jit(solution)/shard_map/broadcast_in_dim | solution.py:105
  (38 shorter events, 32.1 us)
Async XLA Ops:
  6.5 15.6 %copy-start = (bf16[12,128,896]{2,1,0:T(8,128)(2,1)S(1)}, bf16[12,128,896]{2,1,0:T(8,128)(2,1)}, u32[]{:S(2)}) copy-start(bf16[12,128,896]{2,1,0:T(8,128)(2,1)} %param.16) | copy-start | bytes 8257540
  6.5 297.3 %all-gather.2.cloned.1.call-start = ((), (), s32[]{:S(2)}) async-start(), calls=%async_computation.1 | async-start | bytes 17301504 | tf_op jit(solution)/shard_map/all_gather | solution.py:66
  14.1 289.7 %all-to-all-start = ((bf16[32,1,128,2048]{3,2,1,0:T(8,128)(2,1)}), bf16[32,1,128,2048]{3,2,1,0:T(8,128)(2,1)}, u32[]{:S(2)}, u32[]{:S(2)}) async-start(bf16[32,1,128,2048]{3,2,1,0:T(8,128)(2,1)} %stack.2), calls=%async_computation | async-start | bytes 33554432 | tf_op jit(solution)/shard_map/all_to_all | solution.py:64
  31.4 5.0 copy-start.4
  43.6 5.0 copy-start.2
  48.6 255.3 %copy-start.3 = (s32[1,12]{1,0:T(1,128)S(1)}, s32[1,12]{1,0:T(1,128)}, u32[]{:S(2)}) copy-start(s32[1,12]{1,0:T(1,128)} %param.17) | copy-start | bytes 148
  323.4 72.1 %collective-permute-start = (bf16[384,4096]{1,0:T(8,128)(2,1)}, bf16[384,4096]{1,0:T(8,128)(2,1)}, u32[]{:S(2)}, u32[]{:S(2)}) collective-permute-start(bf16[384,4096]{1,0:T(8,128)(2,1)} %broadcast_select_fusion), channel_id=1, source_target_pairs={{0,1},{1,2},{2,3},{4,5},{5,6},{6,7},{8,9},{9,10},{10,11},{12,13},{... | collective-permute-start | bytes 9437192 | tf_op jit(solution)/shard_map/ppermute | solution.py:17
  422.3 71.3 %collective-permute-start.1 = (bf16[384,4096]{1,0:T(8,128)(2,1)}, bf16[384,4096]{1,0:T(8,128)(2,1)}, u32[]{:S(2)}, u32[]{:S(2)}) collective-permute-start(bf16[384,4096]{1,0:T(8,128)(2,1)} %broadcast_select_fusion.1), channel_id=1, source_target_pairs={{0,1},{1,2},{2,3},{4,5},{5,6},{6,7},{8,9},{9,10},{10,11},{12,13},{... | collective-permute-start | bytes 9437192 | tf_op jit(solution)/shard_map/ppermute | solution.py:17
  520.5 244.6 %collective-permute-start.2 = (bf16[384,4096]{1,0:T(8,128)(2,1)}, bf16[384,4096]{1,0:T(8,128)(2,1)}, u32[]{:S(2)}, u32[]{:S(2)}) collective-permute-start(bf16[384,4096]{1,0:T(8,128)(2,1)} %broadcast_select_fusion.2), channel_id=1, source_target_pairs={{0,1},{1,2},{2,3},{4,5},{5,6},{6,7},{8,9},{9,10},{10,11},{12,13},{... | collective-permute-start | bytes 9437192 | tf_op jit(solution)/shard_map/ppermute | solution.py:17
  842.5 15.6 %copy-start.1 = (bf16[12,128,896]{2,1,0:T(8,128)(2,1)S(1)}, bf16[12,128,896]{2,1,0:T(8,128)(2,1)}, u32[]{:S(2)}) copy-start(bf16[12,128,896]{2,1,0:T(8,128)(2,1)} %param.16) | copy-start | bytes 8257540
Sparse Core Ops, SparseCore 0:
  9.5 266.1 all-gather.1
